TPU v7x, 256 devices: a whole 4x4x8 slice. The times are simulated.
256 devices in a mesh: rows: 4 (over y), half: 2 (over core), obs: 32 (over z, x).
Axes of the slice: x: 4, y: 4, z: 8, core: 2. Of those that a mesh axis runs over, the one named last changes fastest.
Arguments:
- ens_state: bfloat16 [2, 8192, 256], P('half', ('rows', 'obs')), may hold values from -6 to 6
- state_pos: bfloat16 [8192], P(('rows', 'obs')), may hold values from 0 to 1
- obs_ens: bfloat16 [2, 2, 65536, 256], P(None, 'half', ('rows', 'obs')), may hold values from -6 to 6
- obs_pos: bfloat16 [2, 65536], P(None, ('rows', 'obs')), may hold values from 0 to 1
- innov_weight: bfloat16 [2, 2, 65536, 256], P(None, 'half', ('rows', 'obs')), may hold values from -0.875 to 0.875
- block_rows: int32 [2, 512, 16], replicated, may hold values from 0 to 63, as said below
Outputs:
- increment: float32 [2, 8192, 256], P('half', ('rows', 'obs'))
Inputs may be any that keep to these rules, and one draw needn't show every extreme that they name: `block_rows`: each row lists 16 different state blocks. Counting state blocks in aligned ranges of 16, an observation block names at most 8 blocks of one range, and in every aligned group of 16 observation blocks some range is named exactly 8 times by each block of the group.
All inputs are finite; a program needn't handle non-finite values.
Results may differ from a plain program's by a relative error of at most 0.0029.
Values may be sent and summed in bfloat16 or wider, within the bound.
No kernel may reach another device: no remote copies, remote signals or barrier semaphores. Data moves between devices by JAX's collectives and lax.ppermute only.
A program may use at most 64 MiB of HBM per device.

v0:
```python
import functools
import math

import jax
import jax.numpy as jnp
from jax import lax
from jax.experimental import pallas as pl
from jax.experimental.pallas import tpu as pltpu
from jax.sharding import PartitionSpec as P


BATCHES = 2
ROWS, HALVES, OBS = 4, 2, 32
NX, NZ = 4, 8
EDGE = 128
SHARD = 64
MEMBERS = 256
RANGE_BLOCKS = 16
SPAN = 4
NAMED = 16
OBS_ROWS = SPAN * EDGE
PAD = 16
Z_ORDER = (0, 1, 4, 5, 2, 3, 6, 7)

TURNS = (0, ROWS - 1, 1, 2)
SPAN_KEYS = BATCHES * RANGE_BLOCKS
DEAD = -1e30
LIVE = math.log2(1.0 / (MEMBERS - 1))
STRETCH = 2.0 * math.sqrt(math.log2(math.e))

VMEM = pl.BlockSpec(memory_space=pltpu.VMEM)


def flip(value):
    return lax.ppermute(value, "half", [(0, 1), (1, 0)])


def along_rows(value, step):
    return lax.ppermute(value, "rows", [(s, (s + step) % ROWS) for s in range(ROWS)])


def along_rows_flip(value, step):
    pairs = [
        (r * HALVES + h, ((r + step) % ROWS) * HALVES + 1 - h)
        for r in range(ROWS)
        for h in range(HALVES)
    ]
    return lax.ppermute(value, ("rows", "half"), pairs)


def swap_z(value, mask):
    pairs = [(z * NX + x, (z ^ mask) * NX + x) for z in range(NZ) for x in range(NX)]
    return lax.ppermute(value, "obs", pairs)


def swap_z_flip(value, mask):
    pairs = [
        (h * OBS + z * NX + x, (1 - h) * OBS + (z ^ mask) * NX + x)
        for h in range(HALVES)
        for z in range(NZ)
        for x in range(NX)
    ]
    return lax.ppermute(value, ("half", "obs"), pairs)


def swap_x(value, mask):
    pairs = [(z * NX + x, z * NX + (x ^ mask)) for z in range(NZ) for x in range(NX)]
    return lax.ppermute(value, "obs", pairs)


def masks_kernel(named, masks, hits):
    row, column = lax.axis_index("rows"), lax.axis_index("obs")
    blocks = lax.broadcasted_iota(jnp.int32, (RANGE_BLOCKS, EDGE), 0) + row * RANGE_BLOCKS
    for chunk in range(ROWS):
        for t in range(BATCHES):
            hit = jnp.zeros((RANGE_BLOCKS, EDGE), jnp.float32)
            for e in range(NAMED):
                picked = named[t, e : e + 1, chunk * EDGE : (chunk + 1) * EDGE]
                hit = jnp.where(picked == blocks, 1.0, hit)
            hits[chunk, t * RANGE_BLOCKS : (t + 1) * RANGE_BLOCKS] = hit
    shift = jnp.bitwise_and(EDGE - column * SPAN, EDGE - 1)
    for k, turn in enumerate(TURNS):
        chunk = hits[jnp.bitwise_and(row + turn, ROWS - 1)]
        rolled = pltpu.roll(chunk, shift, 1)
        for j in range(SPAN):
            wide = jnp.broadcast_to(rolled[:, j : j + 1], (SPAN_KEYS, EDGE))
            masks[k * SPAN_KEYS : (k + 1) * SPAN_KEYS, j * EDGE : (j + 1) * EDGE] = jnp.where(
                wide > 0.5, LIVE, DEAD
            )


def make_masks(named):
    return pl.pallas_call(
        masks_kernel,
        out_shape=jax.ShapeDtypeStruct((len(TURNS) * SPAN_KEYS, SPAN * EDGE), jnp.float32),
        in_specs=[VMEM],
        out_specs=VMEM,
        scratch_shapes=[pltpu.VMEM((ROWS, SPAN_KEYS, EDGE), jnp.float32)],
        compiler_params=pltpu.CompilerParams(vmem_limit_bytes=4 << 20),
        cost_estimate=pl.CostEstimate(flops=4_000_000, transcendentals=0, bytes_accessed=4_000_000),
        name="masks",
    )(named)


def tile_pass(segments, mask, piece, spot, places, tiles, masks, base, out):
    column = lax.axis_index("obs")
    my_z = lax.shift_right_logical(column, 2)
    x = jnp.bitwise_xor(jnp.bitwise_and(column, NX - 1), mask)
    parity = lax.shift_right_logical(x, 1)
    blocks = [2 * jnp.bitwise_xor(my_z, z) + parity for z in Z_ORDER]
    rows = NZ * SHARD
    pair = 2 * EDGE

    def make(spans, buffer):
        for u, (key, place, obs) in enumerate(spans):
            for h in range(SPAN // 2):
                here = obs[h * pair : (h + 1) * pair, :]
                products = lax.dot_general(
                    piece[:rows, :], here, (((1,), (1,)), ((), ())),
                    preferred_element_type=jnp.float32,
                )
                for p, block in enumerate(blocks):
                    part_rows = slice(p * SHARD, (p + 1) * SHARD)
                    positions = spot[part_rows]
                    live = masks[pl.ds(key + block, 1), h * pair : (h + 1) * pair]
                    for i in range(2):
                        j = 2 * h + i
                        lanes = slice(i * EDGE, (i + 1) * EDGE)
                        d = positions - places[place + j : place + j + 1, :]
                        damped = products[part_rows, lanes] * jnp.exp2(live[:, lanes] - d * d)
                        at = (u * SPAN + j) * EDGE
                        tiles[buffer, part_rows, at : at + EDGE] = damped.astype(jnp.bfloat16)

    def add(weights, buffer, first):
        start = 0
        total = None
        for weight in weights:
            depth = weight.shape[0]
            part = jnp.dot(
                tiles[buffer, :, start : start + depth], weight[...],
                preferred_element_type=jnp.float32,
            )
            total = part if total is None else total + part
            start += depth
        if not first:
            total = out[...] + total
        elif base is not None:
            total = base[...] + total
        out[...] = total.astype(out.dtype)

    for n, (spans, weights) in enumerate(segments):
        if n:
            add(segments[n - 1][1], (n - 1) % 2, n == 1)
        make(spans, n % 2)
    last = len(segments) - 1
    add(segments[last][1], last % 2, last == 0)


def spread_places(held, places, start):
    places[start : start + SPAN] = held.astype(jnp.float32)[:SPAN] * STRETCH


def near_kernel(mask, masks, piece, oo, wo, ol, wl, orr, wr, spot, acc, places, tiles):
    lanes = lax.broadcasted_iota(jnp.int32, (SHARD, EDGE), 1)
    sublanes = lax.broadcasted_iota(jnp.int32, (SHARD, EDGE), 0)
    same = lanes == sublanes
    ones = jnp.ones((EDGE, EDGE), jnp.bfloat16)
    held = piece[NZ * SHARD : NZ * SHARD + PAD, :EDGE].astype(jnp.float32)
    spread = jnp.concatenate(
        [jnp.where(same, held[p : p + 1], 0.0) for p in range(NZ)], axis=0
    ).astype(jnp.bfloat16)
    spot[...] = jnp.dot(spread, ones, preferred_element_type=jnp.float32) * STRETCH
    segments = []
    for k, (o, w) in enumerate(((oo, wo), (ol, wl), (orr, wr))):
        spans = []
        for t in range(BATCHES):
            place = (k * BATCHES + t) * SPAN
            spread_places(o[t, OBS_ROWS : OBS_ROWS + PAD, :EDGE], places, place)
            spans.append((k * SPAN_KEYS + t * RANGE_BLOCKS, place, o.at[t]))
        segments.append((spans, (w.reshape(BATCHES * OBS_ROWS, MEMBERS),)))
    tile_pass(segments, mask, piece, spot, places, tiles, masks, None, acc)


SCRATCH = [
    pltpu.VMEM((24, EDGE), jnp.float32),
    pltpu.VMEM((2, NZ * SHARD, BATCHES * SPAN * EDGE), jnp.bfloat16),
]


def near(mask, masks, arrays):
    return pl.pallas_call(
        functools.partial(near_kernel, mask),
        out_shape=(
            jax.ShapeDtypeStruct((NZ * SHARD, EDGE), jnp.float32),
            jax.ShapeDtypeStruct((NZ * SHARD, MEMBERS), jnp.float32),
        ),
        in_specs=[VMEM] * 8,
        out_specs=(VMEM,) * 2,
        scratch_shapes=SCRATCH,
        compiler_params=pltpu.CompilerParams(vmem_limit_bytes=16 << 20),
        cost_estimate=pl.CostEstimate(
            flops=1_000_000_000, transcendentals=1_000_000, bytes_accessed=4_000_000
        ),
    )(masks, *arrays)


def far_kernel(mask, masks, piece, spot, acc, left, right, out, places, tiles):
    spans, weights = [], []
    for t, both in enumerate((left, right)):
        spread_places(both[OBS_ROWS : OBS_ROWS + PAD, :EDGE], places, t * SPAN)
        spans.append(((len(TURNS) - 1) * SPAN_KEYS + t * RANGE_BLOCKS, t * SPAN, both))
        weights.append(both.at[OBS_ROWS + PAD :])
    tile_pass([(spans, weights)], mask, piece, spot, places, tiles, masks, acc, out)


def far(mask, masks, piece, spot, acc, arrays):
    return pl.pallas_call(
        functools.partial(far_kernel, mask),
        out_shape=jax.ShapeDtypeStruct(
            (NZ * SHARD, MEMBERS), jnp.bfloat16 if mask else jnp.float32
        ),
        in_specs=[VMEM] * 6,
        out_specs=VMEM,
        scratch_shapes=SCRATCH,
        compiler_params=pltpu.CompilerParams(vmem_limit_bytes=16 << 20),
        cost_estimate=pl.CostEstimate(
            flops=300_000_000, transcendentals=300_000, bytes_accessed=4_000_000
        ),
    )(masks, piece, spot, acc, *arrays)


def sum_x_kernel(own, x1, x2, x3, keep, send):
    for p in range(NZ):
        rows = slice(p * SHARD, (p + 1) * SHARD)
        total = own[rows]
        for ref in (x1, x2, x3):
            total += ref[rows].astype(jnp.float32)
        out, k = (keep, send)[p & 1], p // 2
        out[k * SHARD : (k + 1) * SHARD] = total.astype(out.dtype)


def sum_pair_kernel(keep, got, own, z4, z2, z6):
    for k, out in enumerate((own, z4, z2, z6)):
        rows = slice(k * SHARD, (k + 1) * SHARD)
        out[...] = (keep[rows] + got[rows].astype(jnp.float32)).astype(out.dtype)


def sum_z_kernel(own, z4, z2, z6, out):
    total = own[...]
    for ref in (z4, z2, z6):
        total += ref[...].astype(jnp.float32)
    out[...] = total


def small(body, out_rows, *arrays):
    return pl.pallas_call(
        body,
        out_shape=tuple(
            jax.ShapeDtypeStruct((rows, MEMBERS), jnp.bfloat16 if n else jnp.float32)
            for n, rows in enumerate(out_rows)
        ),
        in_specs=[VMEM] * len(arrays),
        out_specs=(VMEM,) * len(out_rows),
        compiler_params=pltpu.CompilerParams(vmem_limit_bytes=6 << 20),
    )(*arrays)


def pack_kernel(*refs):
    out = refs[-1]
    held = (refs[0].shape[0] - PAD) // SHARD
    places = []
    for q, ref in enumerate(refs[:-1]):
        for i in range(held):
            p = q * held + i
            out[p * SHARD : (p + 1) * SHARD] = ref[i * SHARD : (i + 1) * SHARD]
        places.append(ref[held * SHARD :].astype(jnp.float32)[:held])
    count = held * (len(refs) - 1)
    places.append(jnp.zeros((PAD - count, MEMBERS), jnp.float32))
    out[count * SHARD :] = jnp.concatenate(places, axis=0).astype(jnp.bfloat16)


def pack(*parts):
    count = len(parts) * (parts[0].shape[0] - PAD) // SHARD
    return pl.pallas_call(
        pack_kernel,
        out_shape=jax.ShapeDtypeStruct((count * SHARD + PAD, MEMBERS), jnp.bfloat16),
        in_specs=[VMEM] * len(parts),
        out_specs=VMEM,
        compiler_params=pltpu.CompilerParams(vmem_limit_bytes=4 << 20),
        name="pack",
    )(*parts)


def load_kernel(
    state_in, state_pos, obs_in, obs_pos, state, obs, state_places, obs_places, sems
):
    copies = [
        pltpu.make_async_copy(state_pos, state_places, sems.at[0]),
        pltpu.make_async_copy(state_in.at[0], state.at[:SHARD], sems.at[1]),
        pltpu.make_async_copy(obs_pos, obs_places, sems.at[2]),
        pltpu.make_async_copy(obs_in.at[0, 0], obs.at[0, :OBS_ROWS], sems.at[3]),
        pltpu.make_async_copy(obs_in.at[1, 0], obs.at[1, :OBS_ROWS], sems.at[4]),
    ]
    for copy in copies:
        copy.start()
    copies[0].wait()
    held = state_places[...].astype(jnp.float32)
    row = jnp.concatenate([held, jnp.zeros((1, MEMBERS - SHARD), jnp.float32)], axis=1)
    rows = jnp.concatenate([row, jnp.zeros((PAD - 1, MEMBERS), jnp.float32)], axis=0)
    state[SHARD:] = rows.astype(jnp.bfloat16)
    copies[2].wait()
    for t in range(BATCHES):
        held = obs_places[t : t + 1].astype(jnp.float32)
        rows = [held[:, r * EDGE : (r + 1) * EDGE] for r in range(SPAN)]
        rows.append(jnp.zeros((PAD - SPAN, EDGE), jnp.float32))
        obs[t, OBS_ROWS:, :EDGE] = jnp.concatenate(rows, axis=0).astype(jnp.bfloat16)
        obs[t, OBS_ROWS:, EDGE:] = jnp.zeros((PAD, MEMBERS - EDGE), jnp.bfloat16)
    for k in (1, 3, 4):
        copies[k].wait()


def load(state, state_pos, obs, obs_pos):
    return pl.pallas_call(
        load_kernel,
        out_shape=(
            jax.ShapeDtypeStruct((SHARD + PAD, MEMBERS), jnp.bfloat16),
            jax.ShapeDtypeStruct((BATCHES, OBS_ROWS + PAD, MEMBERS), jnp.bfloat16),
        ),
        in_specs=[pl.BlockSpec(memory_space=pltpu.HBM)] * 4,
        out_specs=(VMEM, VMEM),
        scratch_shapes=[
            pltpu.VMEM((1, SHARD), jnp.bfloat16),
            pltpu.VMEM((BATCHES, SPAN * EDGE), jnp.bfloat16),
            pltpu.SemaphoreType.DMA((5,)),
        ],
        compiler_params=pltpu.CompilerParams(vmem_limit_bytes=8 << 20),
        name="load",
    )(state, state_pos, obs, obs_pos)


def relay_kernel(batch, obs, weights, out):
    out[: OBS_ROWS + PAD] = obs[batch]
    out[OBS_ROWS + PAD :] = weights[batch]


def relay(batch, obs, weights):
    return pl.pallas_call(
        functools.partial(relay_kernel, batch),
        out_shape=jax.ShapeDtypeStruct((2 * OBS_ROWS + PAD, MEMBERS), jnp.bfloat16),
        in_specs=[VMEM, VMEM],
        out_specs=VMEM,
        compiler_params=pltpu.CompilerParams(vmem_limit_bytes=8 << 20),
        name="relay",
    )(obs, weights)


def local(ens_state, state_pos, obs_ens, obs_pos, innov_weight, block_rows):
    given = (ens_state, state_pos[None], obs_ens, obs_pos)
    state, obs = load(*(pltpu.with_memory_space_constraint(v, pltpu.HBM) for v in given))
    mine = flip(state)
    other = swap_z_flip(state, 1)
    state = pack(mine, other)
    parts = [state]
    for mask in (4, 2, 6):
        parts.append(swap_z(state, mask))
    state = pack(*parts)
    pieces = [state]
    for k in range(1, NX):
        pieces.append(swap_x(state, k))

    weight = innov_weight[:, 0]
    weight_left = along_rows(weight, 1)
    weight_right = along_rows(weight, ROWS - 1)
    obs_left = along_rows_flip(obs, 1)
    obs_right = along_rows_flip(obs, ROWS - 1)
    obs_own = flip(obs)
    far0 = relay(0, obs_left, weight_left)
    far0 = along_rows(far0, 1)
    far1 = relay(1, obs_right, weight_right)
    far1 = along_rows(far1, ROWS - 1)

    masks = make_masks(jnp.transpose(block_rows, (0, 2, 1)))
    seen = (obs_own, weight, obs_left, weight_left, obs_right, weight_right)
    held = []
    for mask in range(NX):
        held.append(near(mask, masks, (pieces[mask], *seen)))
    parts = [None] * NX
    for mask in (2, 3, 1, 0):
        parts[mask] = far(mask, masks, pieces[mask], *held[mask], (far0, far1))
        if mask:
            parts[mask] = swap_x(parts[mask], mask)
    keep, send = small(sum_x_kernel, (4 * SHARD,) * 2, *parts)
    got = swap_z(send, 1)
    own, *parts = small(sum_pair_kernel, (SHARD,) * 4, keep, got)
    for k, mask in enumerate((4, 2, 6)):
        parts[k] = swap_z(parts[k], mask)
    (total,) = small(sum_z_kernel, (SHARD,), own, *parts)
    return total[None]


def solution(mesh):
    in_specs = (
        P("half", ("rows", "obs"), None),
        P(("rows", "obs")),
        P(None, "half", ("rows", "obs"), None),
        P(None, ("rows", "obs")),
        P(None, "half", ("rows", "obs"), None),
        P(),
    )
    out_specs = P("half", ("rows", "obs"), None)
    return jax.shard_map(local, mesh=mesh, in_specs=in_specs, out_specs=out_specs, check_vma=False)
```

profile of v0, /device:TPU:8, one launch (start us, length us, event | category | flops | bytes accessed | tf_op | source)
XLA Modules:
  0.0 92.9 jit_solution(483593086120245912)
XLA Ops:
  0.0 1.6 %collective-permute-start.7 = (bf16[2,512,256]{2,1,0:T(8,128)(2,1)}, bf16[2,512,256]{2,1,0:T(8,128)(2,1)S(1)}, u32[]{:S(2)}, u32[]{:S(2)}) collective-permute-start(bf16[2,512,256]{2,1,0:T(8,128)(2,1)} %bitcast.4), channel_id=1, source_target_pairs={{0,64},{64,128},{128,192},{192,0},{1,65},{65,129},{129,193},{193,1... | collective-permute-start | bytes 1572872 | tf_op jit(solution)/shard_map/ppermute | solution.py:39
  1.6 1.1 %load.1 = (bf16[80,256]{1,0:T(8,128)(2,1)S(1)}, bf16[2,528,256]{2,1,0:T(8,128)(2,1)S(1)}) custom-call(bf16[1,64,256]{2,1,0:T(8,128)(2,1)} %state_in.1, bf16[1,64]{1,0:T(2,128)(2,1)} %bitcast.11, bf16[2,1,512,256]{3,2,1,0:T(8,128)(2,1)} %obs_in.1, bf16[2,512]{1,0:T(2,128)(2,1)} %obs_pos.1), custom_call_target="tpu_custom_call" | custom-call | tf_op jit(solution)/shard_map/load/pallas_call | solution.py:323
  2.7 0.1 collective-permute-start
  2.8 2.0 %collective-permute-start.1 = (bf16[80,256]{1,0:T(8,128)(2,1)S(1)}, bf16[80,256]{1,0:T(8,128)(2,1)S(1)}, u32[]{:S(2)}, u32[]{:S(2)}) collective-permute-start(bf16[80,256]{1,0:T(8,128)(2,1)S(1)} %get-tuple-element.21), channel_id=1, source_target_pairs={{0,36},{1,37},{2,38},{3,39},{4,32},{5,33},{6,34},{7,35},{8,44},{9,... | collective-permute-start | bytes 122888 | tf_op jit(solution)/shard_map/ppermute | solution.py:63
  4.8 1.0 %collective-permute-start.6 = (bf16[2,528,256]{2,1,0:T(8,128)(2,1)S(1)}, bf16[2,528,256]{2,1,0:T(8,128)(2,1)S(1)}, u32[]{:S(2)}, u32[]{:S(2)}) collective-permute-start(bf16[2,528,256]{2,1,0:T(8,128)(2,1)S(1)} %get-tuple-element.22), channel_id=1, source_target_pairs={{0,96},{32,64},{64,160},{96,128},{128,224},{160,192},{192,32},{224... | collective-permute-start | bytes 1622024 | tf_op jit(solution)/shard_map/ppermute | solution.py:48
  5.8 0.8 collective-permute-start.8
  6.6 0.0 collective-permute-done.refs_0_
  6.6 1.7 %collective-permute-start.9 = (bf16[2,512,256]{2,1,0:T(8,128)(2,1)S(1)}, bf16[2,512,256]{2,1,0:T(8,128)(2,1)S(1)}, u32[]{:S(2)}, u32[]{:S(2)}) collective-permute-start(bf16[2,512,256]{2,1,0:T(8,128)(2,1)S(1)} %bitcast.5), channel_id=1, source_target_pairs={{0,192},{64,0},{128,64},{192,128},{1,193},{65,1},{129,65},{193,129... | collective-permute-start | bytes 1572872 | tf_op jit(solution)/shard_map/ppermute | solution.py:39
  8.3 6.4 %collective-permute-start.2 = (bf16[144,256]{1,0:T(8,128)(2,1)S(1)}, bf16[144,256]{1,0:T(8,128)(2,1)S(1)}, u32[]{:S(2)}, u32[]{:S(2)}) collective-permute-start(bf16[144,256]{1,0:T(8,128)(2,1)S(1)} %pack.2.refs_0_), channel_id=1, source_target_pairs={{0,16},{1,17},{2,18},{3,19},{4,20},{5,21},{6,22},{7,23},{8,24},{9,... | collective-permute-start | bytes 221192 | tf_op jit(solution)/shard_map/ppermute | solution.py:53
  14.6 3.4 %collective-permute-done.2.refs_1_ = bf16[144,256]{1,0:T(8,128)(2,1)S(1)} collective-permute-done((bf16[144,256]{1,0:T(8,128)(2,1)S(1)}, bf16[144,256]{1,0:T(8,128)(2,1)S(1)}, u32[]{:S(2)}, u32[]{:S(2)}) %collective-permute-start.2) | collective-permute-done | bytes 73760 | tf_op jit(solution)/shard_map/ppermute | solution.py:53
  18.0 2.9 %collective-permute-start.3 = (bf16[144,256]{1,0:T(8,128)(2,1)S(1)}, bf16[144,256]{1,0:T(8,128)(2,1)S(1)}, u32[]{:S(2)}, u32[]{:S(2)}) collective-permute-start(bf16[144,256]{1,0:T(8,128)(2,1)S(1)} %pack.2.refs_0_), channel_id=1, source_target_pairs={{0,8},{1,9},{2,10},{3,11},{4,12},{5,13},{6,14},{7,15},{8,0},{9,1},... | collective-permute-start | bytes 221192 | tf_op jit(solution)/shard_map/ppermute | solution.py:53
  20.9 3.1 %collective-permute-done.3.refs_2_ = bf16[144,256]{1,0:T(8,128)(2,1)S(1)} collective-permute-done((bf16[144,256]{1,0:T(8,128)(2,1)S(1)}, bf16[144,256]{1,0:T(8,128)(2,1)S(1)}, u32[]{:S(2)}, u32[]{:S(2)}) %collective-permute-start.3) | collective-permute-done | bytes 73760 | tf_op jit(solution)/shard_map/ppermute | solution.py:53
  24.1 4.1 %collective-permute-start.4 = (bf16[144,256]{1,0:T(8,128)(2,1)S(1)}, bf16[144,256]{1,0:T(8,128)(2,1)S(1)}, u32[]{:S(2)}, u32[]{:S(2)}) collective-permute-start(bf16[144,256]{1,0:T(8,128)(2,1)S(1)} %pack.2.refs_0_), channel_id=1, source_target_pairs={{0,24},{1,25},{2,26},{3,27},{4,28},{5,29},{6,30},{7,31},{8,16},{9,... | collective-permute-start | bytes 221192 | tf_op jit(solution)/shard_map/ppermute | solution.py:53
  28.2 2.5 %collective-permute-done.4.refs_3_ = bf16[144,256]{1,0:T(8,128)(2,1)S(1)} collective-permute-done((bf16[144,256]{1,0:T(8,128)(2,1)S(1)}, bf16[144,256]{1,0:T(8,128)(2,1)S(1)}, u32[]{:S(2)}, u32[]{:S(2)}) %collective-permute-start.4) | collective-permute-done | bytes 73760 | tf_op jit(solution)/shard_map/ppermute | solution.py:53
  30.6 0.0 collective-permute-start.5
  30.6 0.0 collective-permute-done.7.wl.weights
  30.7 2.8 %collective-permute-start.16 = (bf16[528,256]{1,0:T(8,128)(2,1)S(1)}, bf16[528,256]{1,0:T(8,128)(2,1)S(1)}, u32[]{:S(2)}, u32[]{:S(2)}) collective-permute-start(bf16[528,256]{1,0:T(8,128)(2,1)S(1)} %pack.3.piece), channel_id=1, source_target_pairs={{0,3},{1,2},{2,1},{3,0},{4,7},{5,6},{6,5},{7,4},{8,11},{9,10},{10,... | collective-permute-start | bytes 811016 | tf_op jit(solution)/shard_map/ppermute | solution.py:68
  33.5 0.0 copy-start.1
  33.6 1.4 %collective-permute-start.10 = (bf16[1040,256]{1,0:T(8,128)(2,1)S(1)}, bf16[1040,256]{1,0:T(8,128)(2,1)S(1)}, u32[]{:S(2)}, u32[]{:S(2)}) collective-permute-start(bf16[1040,256]{1,0:T(8,128)(2,1)S(1)} %relay.2), channel_id=1, source_target_pairs={{0,64},{64,128},{128,192},{192,0},{1,65},{65,129},{129,193},{193,1... | collective-permute-start | bytes 1597448 | tf_op jit(solution)/shard_map/ppermute | solution.py:39
  35.0 0.8 collective-permute-start.11
  35.8 0.8 collective-permute-start.14
  36.6 10.1 %collective-permute-done.16.piece = bf16[528,256]{1,0:T(8,128)(2,1)S(1)} collective-permute-done((bf16[528,256]{1,0:T(8,128)(2,1)S(1)}, bf16[528,256]{1,0:T(8,128)(2,1)S(1)}, u32[]{:S(2)}, u32[]{:S(2)}) %collective-permute-start.16) | collective-permute-done | bytes 270368 | tf_op jit(solution)/shard_map/ppermute | solution.py:68
  46.6 0.3 collective-permute-start.12
  46.9 0.3 masks.1
  47.3 2.0 %shard_map.70 = (f32[512,128]{1,0:T(8,128)S(1)}, f32[512,256]{1,0:T(8,128)S(1)}) custom-call(f32[128,512]{1,0:T(8,128)S(1)} %masks.1, bf16[528,256]{1,0:T(8,128)(2,1)S(1)} %collective-permute-done.16.piece, bf16[2,528,256]{2,1,0:T(8,128)(2,1)S(1)} %collective-permute-done.5.oo, bf16[2,512,256]{2,1,0:T(8,128)(2,1)S(1)} %bitcast.6, ...), custom_call_target="tpu_custom_call" | custom-call | flops 1000000000 | bytes 4000000 | tf_op jit(solution)/shard_map/pallas_call | solution.py:191
  49.3 2.1 %shard_map.68 = (f32[512,128]{1,0:T(8,128)S(1)}, f32[512,256]{1,0:T(8,128)S(1)}) custom-call(f32[128,512]{1,0:T(8,128)S(1)} %masks.1, bf16[528,256]{1,0:T(8,128)(2,1)S(1)} %collective-permute-done.14.piece, bf16[2,528,256]{2,1,0:T(8,128)(2,1)S(1)} %collective-permute-done.5.oo, bf16[2,512,256]{2,1,0:T(8,128)(2,1)S(1)} %bitcast.7, ...), custom_call_target="tpu_custom_call" | custom-call | flops 1000000000 | bytes 4000000 | tf_op jit(solution)/shard_map/pallas_call | solution.py:191
  51.4 3.3 %collective-permute-done.12.piece = bf16[528,256]{1,0:T(8,128)(2,1)S(1)} collective-permute-done((bf16[528,256]{1,0:T(8,128)(2,1)S(1)}, bf16[528,256]{1,0:T(8,128)(2,1)S(1)}, u32[]{:S(2)}, u32[]{:S(2)}) %collective-permute-start.12) | collective-permute-done | bytes 270368 | tf_op jit(solution)/shard_map/ppermute | solution.py:68
  54.7 2.1 %shard_map.66 = (f32[512,128]{1,0:T(8,128)S(1)}, f32[512,256]{1,0:T(8,128)S(1)}) custom-call(f32[128,512]{1,0:T(8,128)S(1)} %masks.1, bf16[528,256]{1,0:T(8,128)(2,1)S(1)} %collective-permute-done.12.piece, bf16[2,528,256]{2,1,0:T(8,128)(2,1)S(1)} %collective-permute-done.5.oo, bf16[2,512,256]{2,1,0:T(8,128)(2,1)S(1)} %bitcast.8, ...), custom_call_target="tpu_custom_call" | custom-call | flops 1000000000 | bytes 4000000 | tf_op jit(solution)/shard_map/pallas_call | solution.py:191
  56.8 1.2 %shard_map.71 = bf16[512,256]{1,0:T(8,128)(2,1)S(1)} custom-call(f32[128,512]{1,0:T(8,128)S(1)} %masks.1, bf16[528,256]{1,0:T(8,128)(2,1)S(1)} %collective-permute-done.16.piece, f32[512,128]{1,0:T(8,128)S(1)} %get-tuple-element.29.spot, f32[512,256]{1,0:T(8,128)S(1)} %get-tuple-element.30.acc, bf16[1040,256]{1,0:T(8,128)(2,1)S(1)} %collective-permute-done.10.left, ...), custom_call_target="tpu_custom_call" | custom-call | flops 300000000 | bytes 4000000 | tf_op jit(solution)/shard_map/pallas_call | solution.py:217
  58.0 2.8 %collective-permute-start.17 = (bf16[512,256]{1,0:T(8,128)(2,1)S(1)}, bf16[512,256]{1,0:T(8,128)(2,1)S(1)}, u32[]{:S(2)}, u32[]{:S(2)}) collective-permute-start(bf16[512,256]{1,0:T(8,128)(2,1)S(1)} %shard_map.71), channel_id=1, source_target_pairs={{0,3},{1,2},{2,1},{3,0},{4,7},{5,6},{6,5},{7,4},{8,11},{9,10},{10,... | collective-permute-start | bytes 786440 | tf_op jit(solution)/shard_map/ppermute | solution.py:68
  60.8 1.2 %shard_map.69 = bf16[512,256]{1,0:T(8,128)(2,1)S(1)} custom-call(f32[128,512]{1,0:T(8,128)S(1)} %masks.1, bf16[528,256]{1,0:T(8,128)(2,1)S(1)} %collective-permute-done.14.piece, f32[512,128]{1,0:T(8,128)S(1)} %get-tuple-element.27.spot, f32[512,256]{1,0:T(8,128)S(1)} %get-tuple-element.28.acc, bf16[1040,256]{1,0:T(8,128)(2,1)S(1)} %collective-permute-done.10.left, ...), custom_call_target="tpu_custom_call" | custom-call | flops 300000000 | bytes 4000000 | tf_op jit(solution)/shard_map/pallas_call | solution.py:217
  62.1 0.1 collective-permute-start.15
  62.2 1.2 %shard_map.67 = bf16[512,256]{1,0:T(8,128)(2,1)S(1)} custom-call(f32[128,512]{1,0:T(8,128)S(1)} %masks.1, bf16[528,256]{1,0:T(8,128)(2,1)S(1)} %collective-permute-done.12.piece, f32[512,128]{1,0:T(8,128)S(1)} %get-tuple-element.25.spot, f32[512,256]{1,0:T(8,128)S(1)} %get-tuple-element.26.acc, bf16[1040,256]{1,0:T(8,128)(2,1)S(1)} %collective-permute-done.10.left, ...), custom_call_target="tpu_custom_call" | custom-call | flops 300000000 | bytes 4000000 | tf_op jit(solution)/shard_map/pallas_call | solution.py:217
  63.4 1.6 %collective-permute-start.13 = (bf16[512,256]{1,0:T(8,128)(2,1)S(1)}, bf16[512,256]{1,0:T(8,128)(2,1)S(1)}, u32[]{:S(2)}, u32[]{:S(2)}) collective-permute-start(bf16[512,256]{1,0:T(8,128)(2,1)S(1)} %shard_map.67), channel_id=1, source_target_pairs={{0,1},{1,0},{2,3},{3,2},{4,5},{5,4},{6,7},{7,6},{8,9},{9,8},{10,11... | collective-permute-start | bytes 786440 | tf_op jit(solution)/shard_map/ppermute | solution.py:68
  65.1 2.1 %shard_map.64 = (f32[512,128]{1,0:T(8,128)S(1)}, f32[512,256]{1,0:T(8,128)S(1)}) custom-call(f32[128,512]{1,0:T(8,128)S(1)} %masks.1, bf16[528,256]{1,0:T(8,128)(2,1)S(1)} %pack.3.piece, bf16[2,528,256]{2,1,0:T(8,128)(2,1)S(1)} %collective-permute-done.5.oo, bf16[2,512,256]{2,1,0:T(8,128)(2,1)S(1)} %bitcast.9, ...), custom_call_target="tpu_custom_call" | custom-call | flops 1000000000 | bytes 4000000 | tf_op jit(solution)/shard_map/pallas_call | solution.py:191
  67.1 1.2 %shard_map.65.own = f32[512,256]{1,0:T(8,128)S(1)} custom-call(f32[128,512]{1,0:T(8,128)S(1)} %masks.1, bf16[528,256]{1,0:T(8,128)(2,1)S(1)} %pack.3.piece, f32[512,128]{1,0:T(8,128)S(1)} %get-tuple-element.23.spot, f32[512,256]{1,0:T(8,128)S(1)} %get-tuple-element.24.acc, bf16[1040,256]{1,0:T(8,128)(2,1)S(1)} %collective-permute-done.10.left, ...), custom_call_target="tpu_custom_call" | custom-call | flops 300000000 | bytes 4000000 | tf_op jit(solution)/shard_map/pallas_call | solution.py:217
  68.4 2.6 %collective-permute-done.17.x3 = bf16[512,256]{1,0:T(8,128)(2,1)S(1)} collective-permute-done((bf16[512,256]{1,0:T(8,128)(2,1)S(1)}, bf16[512,256]{1,0:T(8,128)(2,1)S(1)}, u32[]{:S(2)}, u32[]{:S(2)}) %collective-permute-start.17) | collective-permute-done | bytes 262176 | tf_op jit(solution)/shard_map/ppermute | solution.py:68
  71.0 1.9 %collective-permute-done.15.x2 = bf16[512,256]{1,0:T(8,128)(2,1)S(1)} collective-permute-done((bf16[512,256]{1,0:T(8,128)(2,1)S(1)}, bf16[512,256]{1,0:T(8,128)(2,1)S(1)}, u32[]{:S(2)}, u32[]{:S(2)}) %collective-permute-start.15) | collective-permute-done | bytes 262176 | tf_op jit(solution)/shard_map/ppermute | solution.py:68
  72.9 1.0 %collective-permute-done.13.x1 = bf16[512,256]{1,0:T(8,128)(2,1)S(1)} collective-permute-done((bf16[512,256]{1,0:T(8,128)(2,1)S(1)}, bf16[512,256]{1,0:T(8,128)(2,1)S(1)}, u32[]{:S(2)}, u32[]{:S(2)}) %collective-permute-start.13) | collective-permute-done | bytes 262176 | tf_op jit(solution)/shard_map/ppermute | solution.py:68
  73.9 0.1 shard_map.72
  74.0 0.2 collective-permute-start.18
  74.2 4.8 %collective-permute-done.18.got = bf16[256,256]{1,0:T(8,128)(2,1)S(1)} collective-permute-done((bf16[256,256]{1,0:T(8,128)(2,1)S(1)}, bf16[256,256]{1,0:T(8,128)(2,1)S(1)}, u32[]{:S(2)}, u32[]{:S(2)}) %collective-permute-start.18) | collective-permute-done | bytes 131104 | tf_op jit(solution)/shard_map/ppermute | solution.py:53
  79.1 6.4 %collective-permute-start.19 = (bf16[64,256]{1,0:T(8,128)(2,1)S(1)}, bf16[64,256]{1,0:T(8,128)(2,1)S(1)}, u32[]{:S(2)}, u32[]{:S(2)}) collective-permute-start(bf16[64,256]{1,0:T(8,128)(2,1)S(1)} %get-tuple-element.34), channel_id=1, source_target_pairs={{0,16},{1,17},{2,18},{3,19},{4,20},{5,21},{6,22},{7,23},{8,24},{9,... | collective-permute-start | bytes 98312 | tf_op jit(solution)/shard_map/ppermute | solution.py:53
  85.5 0.7 collective-permute-start.20
  86.2 1.3 %collective-permute-done.19.z4 = bf16[64,256]{1,0:T(8,128)(2,1)S(1)} collective-permute-done((bf16[64,256]{1,0:T(8,128)(2,1)S(1)}, bf16[64,256]{1,0:T(8,128)(2,1)S(1)}, u32[]{:S(2)}, u32[]{:S(2)}) %collective-permute-start.19) | collective-permute-done | bytes 32800 | tf_op jit(solution)/shard_map/ppermute | solution.py:53
  87.5 3.2 %collective-permute-done.20.z2 = bf16[64,256]{1,0:T(8,128)(2,1)S(1)} collective-permute-done((bf16[64,256]{1,0:T(8,128)(2,1)S(1)}, bf16[64,256]{1,0:T(8,128)(2,1)S(1)}, u32[]{:S(2)}, u32[]{:S(2)}) %collective-permute-start.20) | collective-permute-done | bytes 32800 | tf_op jit(solution)/shard_map/ppermute | solution.py:53
  90.7 1.6 %collective-permute-done.21.z6 = bf16[64,256]{1,0:T(8,128)(2,1)S(1)} collective-permute-done((bf16[64,256]{1,0:T(8,128)(2,1)S(1)}, bf16[64,256]{1,0:T(8,128)(2,1)S(1)}, u32[]{:S(2)}, u32[]{:S(2)}) %collective-permute-start.21) | collective-permute-done | bytes 32800 | tf_op jit(solution)/shard_map/ppermute | solution.py:53
  92.2 0.6 shard_map.74
  (17 shorter events, 0.2 us)
Async XLA Ops:
  0.0 6.6 %copy-start = (bf16[2,1,512,256]{3,2,1,0:T(8,128)(2,1)S(1)}, bf16[2,1,512,256]{3,2,1,0:T(8,128)(2,1)}, u32[]{:S(2)}) copy-start(bf16[2,1,512,256]{3,2,1,0:T(8,128)(2,1)} %param.10) | copy-start | bytes 1572868
  0.0 30.6 %collective-permute-start.7 = (bf16[2,512,256]{2,1,0:T(8,128)(2,1)}, bf16[2,512,256]{2,1,0:T(8,128)(2,1)S(1)}, u32[]{:S(2)}, u32[]{:S(2)}) collective-permute-start(bf16[2,512,256]{2,1,0:T(8,128)(2,1)} %bitcast.4), channel_id=1, source_target_pairs={{0,64},{64,128},{128,192},{192,0},{1,65},{65,129},{129,193},{193,1... | collective-permute-start | bytes 1572872 | tf_op jit(solution)/shard_map/ppermute | solution.py:39
  2.7 3.9 %collective-permute-start = (bf16[80,256]{1,0:T(8,128)(2,1)S(1)}, bf16[80,256]{1,0:T(8,128)(2,1)S(1)}, u32[]{:S(2)}, u32[]{:S(2)}) collective-permute-start(bf16[80,256]{1,0:T(8,128)(2,1)S(1)} %get-tuple-element.21), channel_id=1, source_target_pairs={{0,32},{32,0},{1,33},{33,1},{2,34},{34,2},{3,35},{35,3},{4,36},{36... | collective-permute-start | bytes 122888 | tf_op jit(solution)/shard_map/ppermute | solution.py:35
  2.8 5.4 %collective-permute-start.1 = (bf16[80,256]{1,0:T(8,128)(2,1)S(1)}, bf16[80,256]{1,0:T(8,128)(2,1)S(1)}, u32[]{:S(2)}, u32[]{:S(2)}) collective-permute-start(bf16[80,256]{1,0:T(8,128)(2,1)S(1)} %get-tuple-element.21), channel_id=1, source_target_pairs={{0,36},{1,37},{2,38},{3,39},{4,32},{5,33},{6,34},{7,35},{8,44},{9,... | collective-permute-start | bytes 122888 | tf_op jit(solution)/shard_map/ppermute | solution.py:63
  4.8 28.7 %collective-permute-start.6 = (bf16[2,528,256]{2,1,0:T(8,128)(2,1)S(1)}, bf16[2,528,256]{2,1,0:T(8,128)(2,1)S(1)}, u32[]{:S(2)}, u32[]{:S(2)}) collective-permute-start(bf16[2,528,256]{2,1,0:T(8,128)(2,1)S(1)} %get-tuple-element.22), channel_id=1, source_target_pairs={{0,96},{32,64},{64,160},{96,128},{128,224},{160,192},{192,32},{224... | collective-permute-start | bytes 1622024 | tf_op jit(solution)/shard_map/ppermute | solution.py:48
  5.8 29.2 %collective-permute-start.8 = (bf16[2,528,256]{2,1,0:T(8,128)(2,1)S(1)}, bf16[2,528,256]{2,1,0:T(8,128)(2,1)S(1)}, u32[]{:S(2)}, u32[]{:S(2)}) collective-permute-start(bf16[2,528,256]{2,1,0:T(8,128)(2,1)S(1)} %get-tuple-element.22), channel_id=1, source_target_pairs={{0,224},{32,192},{64,32},{96,0},{128,96},{160,64},{192,160},{224,1... | collective-permute-start | bytes 1622024 | tf_op jit(solution)/shard_map/ppermute | solution.py:48
  6.6 28.4 %collective-permute-start.9 = (bf16[2,512,256]{2,1,0:T(8,128)(2,1)S(1)}, bf16[2,512,256]{2,1,0:T(8,128)(2,1)S(1)}, u32[]{:S(2)}, u32[]{:S(2)}) collective-permute-start(bf16[2,512,256]{2,1,0:T(8,128)(2,1)S(1)} %bitcast.5), channel_id=1, source_target_pairs={{0,192},{64,0},{128,64},{192,128},{1,193},{65,1},{129,65},{193,129... | collective-permute-start | bytes 1572872 | tf_op jit(solution)/shard_map/ppermute | solution.py:39
  8.3 9.8 %collective-permute-start.2 = (bf16[144,256]{1,0:T(8,128)(2,1)S(1)}, bf16[144,256]{1,0:T(8,128)(2,1)S(1)}, u32[]{:S(2)}, u32[]{:S(2)}) collective-permute-start(bf16[144,256]{1,0:T(8,128)(2,1)S(1)} %pack.2.refs_0_), channel_id=1, source_target_pairs={{0,16},{1,17},{2,18},{3,19},{4,20},{5,21},{6,22},{7,23},{8,24},{9,... | collective-permute-start | bytes 221192 | tf_op jit(solution)/shard_map/ppermute | solution.py:53
  18.0 6.0 %collective-permute-start.3 = (bf16[144,256]{1,0:T(8,128)(2,1)S(1)}, bf16[144,256]{1,0:T(8,128)(2,1)S(1)}, u32[]{:S(2)}, u32[]{:S(2)}) collective-permute-start(bf16[144,256]{1,0:T(8,128)(2,1)S(1)} %pack.2.refs_0_), channel_id=1, source_target_pairs={{0,8},{1,9},{2,10},{3,11},{4,12},{5,13},{6,14},{7,15},{8,0},{9,1},... | collective-permute-start | bytes 221192 | tf_op jit(solution)/shard_map/ppermute | solution.py:53
  24.1 6.5 %collective-permute-start.4 = (bf16[144,256]{1,0:T(8,128)(2,1)S(1)}, bf16[144,256]{1,0:T(8,128)(2,1)S(1)}, u32[]{:S(2)}, u32[]{:S(2)}) collective-permute-start(bf16[144,256]{1,0:T(8,128)(2,1)S(1)} %pack.2.refs_0_), channel_id=1, source_target_pairs={{0,24},{1,25},{2,26},{3,27},{4,28},{5,29},{6,30},{7,31},{8,16},{9,... | collective-permute-start | bytes 221192 | tf_op jit(solution)/shard_map/ppermute | solution.py:53
  30.6 16.6 %collective-permute-start.5 = (bf16[2,528,256]{2,1,0:T(8,128)(2,1)S(1)}, bf16[2,528,256]{2,1,0:T(8,128)(2,1)S(1)}, u32[]{:S(2)}, u32[]{:S(2)}) collective-permute-start(bf16[2,528,256]{2,1,0:T(8,128)(2,1)S(1)} %get-tuple-element.22), channel_id=1, source_target_pairs={{0,32},{32,0},{1,33},{33,1},{2,34},{34,2},{3,35},{35,3},{4,36},{36... | collective-permute-start | bytes 1622024 | tf_op jit(solution)/shard_map/ppermute | solution.py:35
  30.7 16.0 %collective-permute-start.16 = (bf16[528,256]{1,0:T(8,128)(2,1)S(1)}, bf16[528,256]{1,0:T(8,128)(2,1)S(1)}, u32[]{:S(2)}, u32[]{:S(2)}) collective-permute-start(bf16[528,256]{1,0:T(8,128)(2,1)S(1)} %pack.3.piece), channel_id=1, source_target_pairs={{0,3},{1,2},{2,1},{3,0},{4,7},{5,6},{6,5},{7,4},{8,11},{9,10},{10,... | collective-permute-start | bytes 811016 | tf_op jit(solution)/shard_map/ppermute | solution.py:68
  33.5 13.4 %copy-start.1 = (s32[2,512,16]{1,2,0:T(8,128)S(1)}, s32[2,512,16]{1,2,0:T(8,128)}, u32[]{:S(2)}) copy-start(s32[2,512,16]{1,2,0:T(8,128)} %param.11) | copy-start | bytes 196612
  33.6 23.2 %collective-permute-start.10 = (bf16[1040,256]{1,0:T(8,128)(2,1)S(1)}, bf16[1040,256]{1,0:T(8,128)(2,1)S(1)}, u32[]{:S(2)}, u32[]{:S(2)}) collective-permute-start(bf16[1040,256]{1,0:T(8,128)(2,1)S(1)} %relay.2), channel_id=1, source_target_pairs={{0,64},{64,128},{128,192},{192,0},{1,65},{65,129},{129,193},{193,1... | collective-permute-start | bytes 1597448 | tf_op jit(solution)/shard_map/ppermute | solution.py:39
  35.0 21.7 %collective-permute-start.11 = (bf16[1040,256]{1,0:T(8,128)(2,1)S(1)}, bf16[1040,256]{1,0:T(8,128)(2,1)S(1)}, u32[]{:S(2)}, u32[]{:S(2)}) collective-permute-start(bf16[1040,256]{1,0:T(8,128)(2,1)S(1)} %relay.3), channel_id=1, source_target_pairs={{0,192},{64,0},{128,64},{192,128},{1,193},{65,1},{129,65},{193,129... | collective-permute-start | bytes 1597448 | tf_op jit(solution)/shard_map/ppermute | solution.py:39
  35.8 13.5 %collective-permute-start.14 = (bf16[528,256]{1,0:T(8,128)(2,1)S(1)}, bf16[528,256]{1,0:T(8,128)(2,1)S(1)}, u32[]{:S(2)}, u32[]{:S(2)}) collective-permute-start(bf16[528,256]{1,0:T(8,128)(2,1)S(1)} %pack.3.piece), channel_id=1, source_target_pairs={{0,2},{1,3},{2,0},{3,1},{4,6},{5,7},{6,4},{7,5},{8,10},{9,11},{10,... | collective-permute-start | bytes 811016 | tf_op jit(solution)/shard_map/ppermute | solution.py:68
  46.6 8.0 %collective-permute-start.12 = (bf16[528,256]{1,0:T(8,128)(2,1)S(1)}, bf16[528,256]{1,0:T(8,128)(2,1)S(1)}, u32[]{:S(2)}, u32[]{:S(2)}) collective-permute-start(bf16[528,256]{1,0:T(8,128)(2,1)S(1)} %pack.3.piece), channel_id=1, source_target_pairs={{0,1},{1,0},{2,3},{3,2},{4,5},{5,4},{6,7},{7,6},{8,9},{9,8},{10,11... | collective-permute-start | bytes 811016 | tf_op jit(solution)/shard_map/ppermute | solution.py:68
  58.0 13.0 %collective-permute-start.17 = (bf16[512,256]{1,0:T(8,128)(2,1)S(1)}, bf16[512,256]{1,0:T(8,128)(2,1)S(1)}, u32[]{:S(2)}, u32[]{:S(2)}) collective-permute-start(bf16[512,256]{1,0:T(8,128)(2,1)S(1)} %shard_map.71), channel_id=1, source_target_pairs={{0,3},{1,2},{2,1},{3,0},{4,7},{5,6},{6,5},{7,4},{8,11},{9,10},{10,... | collective-permute-start | bytes 786440 | tf_op jit(solution)/shard_map/ppermute | solution.py:68
  62.1 10.8 %collective-permute-start.15 = (bf16[512,256]{1,0:T(8,128)(2,1)S(1)}, bf16[512,256]{1,0:T(8,128)(2,1)S(1)}, u32[]{:S(2)}, u32[]{:S(2)}) collective-permute-start(bf16[512,256]{1,0:T(8,128)(2,1)S(1)} %shard_map.69), channel_id=1, source_target_pairs={{0,2},{1,3},{2,0},{3,1},{4,6},{5,7},{6,4},{7,5},{8,10},{9,11},{10,... | collective-permute-start | bytes 786440 | tf_op jit(solution)/shard_map/ppermute | solution.py:68
  63.4 10.4 %collective-permute-start.13 = (bf16[512,256]{1,0:T(8,128)(2,1)S(1)}, bf16[512,256]{1,0:T(8,128)(2,1)S(1)}, u32[]{:S(2)}, u32[]{:S(2)}) collective-permute-start(bf16[512,256]{1,0:T(8,128)(2,1)S(1)} %shard_map.67), channel_id=1, source_target_pairs={{0,1},{1,0},{2,3},{3,2},{4,5},{5,4},{6,7},{7,6},{8,9},{9,8},{10,11... | collective-permute-start | bytes 786440 | tf_op jit(solution)/shard_map/ppermute | solution.py:68
  74.0 5.1 %collective-permute-start.18 = (bf16[256,256]{1,0:T(8,128)(2,1)S(1)}, bf16[256,256]{1,0:T(8,128)(2,1)S(1)}, u32[]{:S(2)}, u32[]{:S(2)}) collective-permute-start(bf16[256,256]{1,0:T(8,128)(2,1)S(1)} %get-tuple-element.32), channel_id=1, source_target_pairs={{0,4},{1,5},{2,6},{3,7},{4,0},{5,1},{6,2},{7,3},{8,12},{9,13},{10,... | collective-permute-start | bytes 393224 | tf_op jit(solution)/shard_map/ppermute | solution.py:53
  79.1 8.4 %collective-permute-start.19 = (bf16[64,256]{1,0:T(8,128)(2,1)S(1)}, bf16[64,256]{1,0:T(8,128)(2,1)S(1)}, u32[]{:S(2)}, u32[]{:S(2)}) collective-permute-start(bf16[64,256]{1,0:T(8,128)(2,1)S(1)} %get-tuple-element.34), channel_id=1, source_target_pairs={{0,16},{1,17},{2,18},{3,19},{4,20},{5,21},{6,22},{7,23},{8,24},{9,... | collective-permute-start | bytes 98312 | tf_op jit(solution)/shard_map/ppermute | solution.py:53
  85.5 5.2 %collective-permute-start.20 = (bf16[64,256]{1,0:T(8,128)(2,1)S(1)}, bf16[64,256]{1,0:T(8,128)(2,1)S(1)}, u32[]{:S(2)}, u32[]{:S(2)}) collective-permute-start(bf16[64,256]{1,0:T(8,128)(2,1)S(1)} %get-tuple-element.35), channel_id=1, source_target_pairs={{0,8},{1,9},{2,10},{3,11},{4,12},{5,13},{6,14},{7,15},{8,0},{9,1},... | collective-permute-start | bytes 98312 | tf_op jit(solution)/shard_map/ppermute | solution.py:53
  86.2 6.0 %collective-permute-start.21 = (bf16[64,256]{1,0:T(8,128)(2,1)S(1)}, bf16[64,256]{1,0:T(8,128)(2,1)S(1)}, u32[]{:S(2)}, u32[]{:S(2)}) collective-permute-start(bf16[64,256]{1,0:T(8,128)(2,1)S(1)} %get-tuple-element.36), channel_id=1, source_target_pairs={{0,24},{1,25},{2,26},{3,27},{4,28},{5,29},{6,30},{7,31},{8,16},{9,... | collective-permute-start | bytes 98312 | tf_op jit(solution)/shard_map/ppermute | solution.py:53
where the time goes:
time: 93 us; the launch traced here: 92.9 us
  waiting for transfers between devices  38.7 us (42%)
  starting transfers between devices  38.5 us (41%)
  Pallas kernels  15.5 us (17%)
    ppermute x7, starting transfers between devices, swap_z(): return lax.ppermute(value, 'obs', pairs)  20.7 us
    ppermute x7, waiting for transfers between devices, swap_z(): return lax.ppermute(value, 'obs', pairs)  19.8 us
    ppermute x6, waiting for transfers between devices, swap_x(): return lax.ppermute(value, 'obs', pairs)  18.9 us
    ppermute x6, starting transfers between devices, swap_x(): return lax.ppermute(value, 'obs', pairs)  8.49 us
    pallas_call x4, Pallas kernels, near(): pl.pallas_call(functools.partial(near_kernel, mask), out_shape=(jax.Shape...  8.24 us
    ppermute x4, starting transfers between devices, along_rows(): lax.ppermute(value, 'rows', [(s, (s + step) % ROWS) for s in range(ROWS)])  5.42 us
    pallas_call x4, Pallas kernels, far(): pl.pallas_call(functools.partial(far_kernel, mask), out_shape=jax.ShapeDt...  4.95 us
    ppermute x1, starting transfers between devices, swap_z_flip(): return lax.ppermute(value, ('half', 'obs'), pairs)  2.02 us
  transfers between devices with their start and end apart: 22, of which 12 were waited for; matrix products, arithmetic and copies ran while one was open for 0% of the time, Pallas kernels for 15%

commit v1 on v0

--- a/solution.py
+++ b/solution.py
@@ -102,7 +102,7 @@
     )(named)
 
 
-def tile_pass(segments, mask, piece, spot, places, tiles, masks, base, out):
+def tile_pass(segments, mask, piece, spot, places, tiles, masks, base, held, out):
     column = lax.axis_index("obs")
     my_z = lax.shift_right_logical(column, 2)
     x = jnp.bitwise_xor(jnp.bitwise_and(column, NX - 1), mask)
@@ -131,29 +131,23 @@
                         at = (u * SPAN + j) * EDGE
                         tiles[buffer, part_rows, at : at + EDGE] = damped.astype(jnp.bfloat16)
 
-    def add(weights, buffer, first):
-        start = 0
-        total = None
-        for weight in weights:
-            depth = weight.shape[0]
-            part = jnp.dot(
-                tiles[buffer, :, start : start + depth], weight[...],
-                preferred_element_type=jnp.float32,
-            )
-            total = part if total is None else total + part
-            start += depth
+    def add(weight, buffer, first, out):
+        depth = weight.shape[0]
+        total = jnp.dot(
+            tiles[buffer, :, :depth], weight[...], preferred_element_type=jnp.float32
+        )
         if not first:
-            total = out[...] + total
+            total = held[...] + total
         elif base is not None:
             total = base[...] + total
         out[...] = total.astype(out.dtype)
 
-    for n, (spans, weights) in enumerate(segments):
+    for n, (spans, weight) in enumerate(segments):
         if n:
-            add(segments[n - 1][1], (n - 1) % 2, n == 1)
+            add(segments[n - 1][1], (n - 1) % 2, n == 1, held)
         make(spans, n % 2)
     last = len(segments) - 1
-    add(segments[last][1], last % 2, last == 0)
+    add(segments[last][1], last % 2, last == 0, out)
 
 
 def spread_places(held, places, start):
@@ -177,8 +171,8 @@
             place = (k * BATCHES + t) * SPAN
             spread_places(o[t, OBS_ROWS : OBS_ROWS + PAD, :EDGE], places, place)
             spans.append((k * SPAN_KEYS + t * RANGE_BLOCKS, place, o.at[t]))
-        segments.append((spans, (w.reshape(BATCHES * OBS_ROWS, MEMBERS),)))
-    tile_pass(segments, mask, piece, spot, places, tiles, masks, None, acc)
+        segments.append((spans, w.reshape(BATCHES * OBS_ROWS, MEMBERS)))
+    tile_pass(segments, mask, piece, spot, places, tiles, masks, None, acc, acc)
 
 
 SCRATCH = [
@@ -204,13 +198,13 @@
     )(masks, *arrays)
 
 
-def far_kernel(mask, masks, piece, spot, acc, left, right, out, places, tiles):
-    spans, weights = [], []
+def far_kernel(mask, masks, piece, spot, acc, left, right, out, places, tiles, held):
+    segments = []
     for t, both in enumerate((left, right)):
         spread_places(both[OBS_ROWS : OBS_ROWS + PAD, :EDGE], places, t * SPAN)
-        spans.append(((len(TURNS) - 1) * SPAN_KEYS + t * RANGE_BLOCKS, t * SPAN, both))
-        weights.append(both.at[OBS_ROWS + PAD :])
-    tile_pass([(spans, weights)], mask, piece, spot, places, tiles, masks, acc, out)
+        span = ((len(TURNS) - 1) * SPAN_KEYS + t * RANGE_BLOCKS, t * SPAN, both)
+        segments.append(([span], both.at[OBS_ROWS + PAD :]))
+    tile_pass(segments, mask, piece, spot, places, tiles, masks, acc, held, out)
 
 
 def far(mask, masks, piece, spot, acc, arrays):
@@ -221,7 +215,7 @@
         ),
         in_specs=[VMEM] * 6,
         out_specs=VMEM,
-        scratch_shapes=SCRATCH,
+        scratch_shapes=SCRATCH + [pltpu.VMEM((NZ * SHARD, MEMBERS), jnp.float32)],
         compiler_params=pltpu.CompilerParams(vmem_limit_bytes=16 << 20),
         cost_estimate=pl.CostEstimate(
             flops=300_000_000, transcendentals=300_000, bytes_accessed=4_000_000
@@ -385,7 +379,7 @@
     for mask in range(NX):
         held.append(near(mask, masks, (pieces[mask], *seen)))
     parts = [None] * NX
-    for mask in (2, 3, 1, 0):
+    for mask in (1, 3, 2, 0):
         parts[mask] = far(mask, masks, pieces[mask], *held[mask], (far0, far1))
         if mask:
             parts[mask] = swap_x(parts[mask], mask)

time: 93 us -> 92.6 us (level)
  the two profiles are of different devices: /device:TPU:8 before, /device:TPU:14 now
where the time goes in v1:
time: 92.6 us; the launch traced here: 92.5 us
  waiting for transfers between devices  39.8 us (43%)
  starting transfers between devices  37.8 us (41%)
  Pallas kernels  14.8 us (16%)
    ppermute x7, starting transfers between devices, swap_z(): return lax.ppermute(value, 'obs', pairs)  20.9 us
    ppermute x6, waiting for transfers between devices, swap_x(): return lax.ppermute(value, 'obs', pairs)  20.1 us
    ppermute x7, waiting for transfers between devices, swap_z(): return lax.ppermute(value, 'obs', pairs)  19.7 us
    pallas_call x4, Pallas kernels, near(): pl.pallas_call(functools.partial(near_kernel, mask), out_shape=(jax.Shape...  8.24 us
    ppermute x6, starting transfers between devices, swap_x(): return lax.ppermute(value, 'obs', pairs)  7.56 us
    ppermute x4, starting transfers between devices, along_rows(): lax.ppermute(value, 'rows', [(s, (s + step) % ROWS) for s in range(ROWS)])  5.42 us
    pallas_call x4, Pallas kernels, far(): pl.pallas_call(functools.partial(far_kernel, mask), out_shape=jax.ShapeDt...  4.23 us
    ppermute x1, starting transfers between devices, swap_z_flip(): return lax.ppermute(value, ('half', 'obs'), pairs)  2.02 us
  transfers between devices with their start and end apart: 22, of which 11 were waited for; matrix products, arithmetic and copies ran while one was open for 0% of the time, Pallas kernels for 14%

profile of v1, /device:TPU:14, one launch (start us, length us, event | category | flops | bytes accessed | tf_op | source)
XLA Modules:
  0.0 92.5 jit_solution(17055981545536530372)
XLA Ops:
  0.0 1.6 %collective-permute-start.7 = (bf16[2,512,256]{2,1,0:T(8,128)(2,1)}, bf16[2,512,256]{2,1,0:T(8,128)(2,1)S(1)}, u32[]{:S(2)}, u32[]{:S(2)}) collective-permute-start(bf16[2,512,256]{2,1,0:T(8,128)(2,1)} %bitcast.4), channel_id=1, source_target_pairs={{0,64},{64,128},{128,192},{192,0},{1,65},{65,129},{129,193},{193,1... | collective-permute-start | bytes 1572872 | tf_op jit(solution)/shard_map/ppermute | solution.py:39
  1.6 1.1 %load.1 = (bf16[80,256]{1,0:T(8,128)(2,1)S(1)}, bf16[2,528,256]{2,1,0:T(8,128)(2,1)S(1)}) custom-call(bf16[1,64,256]{2,1,0:T(8,128)(2,1)} %state_in.1, bf16[1,64]{1,0:T(2,128)(2,1)} %bitcast.11, bf16[2,1,512,256]{3,2,1,0:T(8,128)(2,1)} %obs_in.1, bf16[2,512]{1,0:T(2,128)(2,1)} %obs_pos.1), custom_call_target="tpu_custom_call" | custom-call | tf_op jit(solution)/shard_map/load/pallas_call | solution.py:317
  2.7 0.1 collective-permute-start
  2.8 2.0 %collective-permute-start.1 = (bf16[80,256]{1,0:T(8,128)(2,1)S(1)}, bf16[80,256]{1,0:T(8,128)(2,1)S(1)}, u32[]{:S(2)}, u32[]{:S(2)}) collective-permute-start(bf16[80,256]{1,0:T(8,128)(2,1)S(1)} %get-tuple-element.21), channel_id=1, source_target_pairs={{0,36},{1,37},{2,38},{3,39},{4,32},{5,33},{6,34},{7,35},{8,44},{9,... | collective-permute-start | bytes 122888 | tf_op jit(solution)/shard_map/ppermute | solution.py:63
  4.8 1.0 %collective-permute-start.6 = (bf16[2,528,256]{2,1,0:T(8,128)(2,1)S(1)}, bf16[2,528,256]{2,1,0:T(8,128)(2,1)S(1)}, u32[]{:S(2)}, u32[]{:S(2)}) collective-permute-start(bf16[2,528,256]{2,1,0:T(8,128)(2,1)S(1)} %get-tuple-element.22), channel_id=1, source_target_pairs={{0,96},{32,64},{64,160},{96,128},{128,224},{160,192},{192,32},{224... | collective-permute-start | bytes 1622024 | tf_op jit(solution)/shard_map/ppermute | solution.py:48
  5.8 0.8 collective-permute-start.8
  6.6 0.0 collective-permute-done.refs_0_
  6.6 1.7 %collective-permute-start.9 = (bf16[2,512,256]{2,1,0:T(8,128)(2,1)S(1)}, bf16[2,512,256]{2,1,0:T(8,128)(2,1)S(1)}, u32[]{:S(2)}, u32[]{:S(2)}) collective-permute-start(bf16[2,512,256]{2,1,0:T(8,128)(2,1)S(1)} %bitcast.5), channel_id=1, source_target_pairs={{0,192},{64,0},{128,64},{192,128},{1,193},{65,1},{129,65},{193,129... | collective-permute-start | bytes 1572872 | tf_op jit(solution)/shard_map/ppermute | solution.py:39
  8.3 6.4 %collective-permute-start.2 = (bf16[144,256]{1,0:T(8,128)(2,1)S(1)}, bf16[144,256]{1,0:T(8,128)(2,1)S(1)}, u32[]{:S(2)}, u32[]{:S(2)}) collective-permute-start(bf16[144,256]{1,0:T(8,128)(2,1)S(1)} %pack.2.refs_0_), channel_id=1, source_target_pairs={{0,16},{1,17},{2,18},{3,19},{4,20},{5,21},{6,22},{7,23},{8,24},{9,... | collective-permute-start | bytes 221192 | tf_op jit(solution)/shard_map/ppermute | solution.py:53
  14.6 3.4 %collective-permute-done.2.refs_1_ = bf16[144,256]{1,0:T(8,128)(2,1)S(1)} collective-permute-done((bf16[144,256]{1,0:T(8,128)(2,1)S(1)}, bf16[144,256]{1,0:T(8,128)(2,1)S(1)}, u32[]{:S(2)}, u32[]{:S(2)}) %collective-permute-start.2) | collective-permute-done | bytes 73760 | tf_op jit(solution)/shard_map/ppermute | solution.py:53
  18.0 2.9 %collective-permute-start.3 = (bf16[144,256]{1,0:T(8,128)(2,1)S(1)}, bf16[144,256]{1,0:T(8,128)(2,1)S(1)}, u32[]{:S(2)}, u32[]{:S(2)}) collective-permute-start(bf16[144,256]{1,0:T(8,128)(2,1)S(1)} %pack.2.refs_0_), channel_id=1, source_target_pairs={{0,8},{1,9},{2,10},{3,11},{4,12},{5,13},{6,14},{7,15},{8,0},{9,1},... | collective-permute-start | bytes 221192 | tf_op jit(solution)/shard_map/ppermute | solution.py:53
  20.9 3.1 %collective-permute-done.3.refs_2_ = bf16[144,256]{1,0:T(8,128)(2,1)S(1)} collective-permute-done((bf16[144,256]{1,0:T(8,128)(2,1)S(1)}, bf16[144,256]{1,0:T(8,128)(2,1)S(1)}, u32[]{:S(2)}, u32[]{:S(2)}) %collective-permute-start.3) | collective-permute-done | bytes 73760 | tf_op jit(solution)/shard_map/ppermute | solution.py:53
  24.1 4.1 %collective-permute-start.4 = (bf16[144,256]{1,0:T(8,128)(2,1)S(1)}, bf16[144,256]{1,0:T(8,128)(2,1)S(1)}, u32[]{:S(2)}, u32[]{:S(2)}) collective-permute-start(bf16[144,256]{1,0:T(8,128)(2,1)S(1)} %pack.2.refs_0_), channel_id=1, source_target_pairs={{0,24},{1,25},{2,26},{3,27},{4,28},{5,29},{6,30},{7,31},{8,16},{9,... | collective-permute-start | bytes 221192 | tf_op jit(solution)/shard_map/ppermute | solution.py:53
  28.2 2.5 %collective-permute-done.4.refs_3_ = bf16[144,256]{1,0:T(8,128)(2,1)S(1)} collective-permute-done((bf16[144,256]{1,0:T(8,128)(2,1)S(1)}, bf16[144,256]{1,0:T(8,128)(2,1)S(1)}, u32[]{:S(2)}, u32[]{:S(2)}) %collective-permute-start.4) | collective-permute-done | bytes 73760 | tf_op jit(solution)/shard_map/ppermute | solution.py:53
  30.6 0.0 collective-permute-start.5
  30.6 0.0 collective-permute-done.7.wl.weights
  30.7 0.6 collective-permute-start.16
  31.2 0.0 collective-permute-done.6.ol.obs
  31.3 0.0 copy-start.1
  31.3 1.4 %collective-permute-start.10 = (bf16[1040,256]{1,0:T(8,128)(2,1)S(1)}, bf16[1040,256]{1,0:T(8,128)(2,1)S(1)}, u32[]{:S(2)}, u32[]{:S(2)}) collective-permute-start(bf16[1040,256]{1,0:T(8,128)(2,1)S(1)} %relay.2), channel_id=1, source_target_pairs={{0,64},{64,128},{128,192},{192,0},{1,65},{65,129},{129,193},{193,1... | collective-permute-start | bytes 1597448 | tf_op jit(solution)/shard_map/ppermute | solution.py:39
  32.7 0.8 collective-permute-start.11
  33.5 2.4 %collective-permute-start.14 = (bf16[528,256]{1,0:T(8,128)(2,1)S(1)}, bf16[528,256]{1,0:T(8,128)(2,1)S(1)}, u32[]{:S(2)}, u32[]{:S(2)}) collective-permute-start(bf16[528,256]{1,0:T(8,128)(2,1)S(1)} %pack.3.piece), channel_id=1, source_target_pairs={{0,2},{1,3},{2,0},{3,1},{4,6},{5,7},{6,4},{7,5},{8,10},{9,11},{10,... | collective-permute-start | bytes 811016 | tf_op jit(solution)/shard_map/ppermute | solution.py:68
  35.9 10.7 %collective-permute-done.16.piece = bf16[528,256]{1,0:T(8,128)(2,1)S(1)} collective-permute-done((bf16[528,256]{1,0:T(8,128)(2,1)S(1)}, bf16[528,256]{1,0:T(8,128)(2,1)S(1)}, u32[]{:S(2)}, u32[]{:S(2)}) %collective-permute-start.16) | collective-permute-done | bytes 270368 | tf_op jit(solution)/shard_map/ppermute | solution.py:68
  46.6 0.0 collective-permute-start.12
  46.6 0.3 masks.1
  47.0 2.0 %shard_map.70 = (f32[512,128]{1,0:T(8,128)S(1)}, f32[512,256]{1,0:T(8,128)S(1)}) custom-call(f32[128,512]{1,0:T(8,128)S(1)} %masks.1, bf16[528,256]{1,0:T(8,128)(2,1)S(1)} %collective-permute-done.16.piece, bf16[2,528,256]{2,1,0:T(8,128)(2,1)S(1)} %collective-permute-done.5.oo, bf16[2,512,256]{2,1,0:T(8,128)(2,1)S(1)} %bitcast.6, ...), custom_call_target="tpu_custom_call" | custom-call | flops 1000000000 | bytes 4000000 | tf_op jit(solution)/shard_map/pallas_call | solution.py:185
  49.0 2.1 %shard_map.68 = (f32[512,128]{1,0:T(8,128)S(1)}, f32[512,256]{1,0:T(8,128)S(1)}) custom-call(f32[128,512]{1,0:T(8,128)S(1)} %masks.1, bf16[528,256]{1,0:T(8,128)(2,1)S(1)} %collective-permute-done.14.piece, bf16[2,528,256]{2,1,0:T(8,128)(2,1)S(1)} %collective-permute-done.5.oo, bf16[2,512,256]{2,1,0:T(8,128)(2,1)S(1)} %bitcast.7, ...), custom_call_target="tpu_custom_call" | custom-call | flops 1000000000 | bytes 4000000 | tf_op jit(solution)/shard_map/pallas_call | solution.py:185
  51.1 3.6 %collective-permute-done.12.piece = bf16[528,256]{1,0:T(8,128)(2,1)S(1)} collective-permute-done((bf16[528,256]{1,0:T(8,128)(2,1)S(1)}, bf16[528,256]{1,0:T(8,128)(2,1)S(1)}, u32[]{:S(2)}, u32[]{:S(2)}) %collective-permute-start.12) | collective-permute-done | bytes 270368 | tf_op jit(solution)/shard_map/ppermute | solution.py:68
  54.7 2.1 %shard_map.66 = (f32[512,128]{1,0:T(8,128)S(1)}, f32[512,256]{1,0:T(8,128)S(1)}) custom-call(f32[128,512]{1,0:T(8,128)S(1)} %masks.1, bf16[528,256]{1,0:T(8,128)(2,1)S(1)} %collective-permute-done.12.piece, bf16[2,528,256]{2,1,0:T(8,128)(2,1)S(1)} %collective-permute-done.5.oo, bf16[2,512,256]{2,1,0:T(8,128)(2,1)S(1)} %bitcast.8, ...), custom_call_target="tpu_custom_call" | custom-call | flops 1000000000 | bytes 4000000 | tf_op jit(solution)/shard_map/pallas_call | solution.py:185
  56.8 1.1 %shard_map.71 = bf16[512,256]{1,0:T(8,128)(2,1)S(1)} custom-call(f32[128,512]{1,0:T(8,128)S(1)} %masks.1, bf16[528,256]{1,0:T(8,128)(2,1)S(1)} %collective-permute-done.16.piece, f32[512,128]{1,0:T(8,128)S(1)} %get-tuple-element.29.spot, f32[512,256]{1,0:T(8,128)S(1)} %get-tuple-element.30.acc, bf16[1040,256]{1,0:T(8,128)(2,1)S(1)} %collective-permute-done.10.left, ...), custom_call_target="tpu_custom_call" | custom-call | flops 300000000 | bytes 4000000 | tf_op jit(solution)/shard_map/pallas_call | solution.py:211
  57.8 0.6 collective-permute-start.17
  58.4 1.1 %shard_map.69 = bf16[512,256]{1,0:T(8,128)(2,1)S(1)} custom-call(f32[128,512]{1,0:T(8,128)S(1)} %masks.1, bf16[528,256]{1,0:T(8,128)(2,1)S(1)} %collective-permute-done.14.piece, f32[512,128]{1,0:T(8,128)S(1)} %get-tuple-element.27.spot, f32[512,256]{1,0:T(8,128)S(1)} %get-tuple-element.28.acc, bf16[1040,256]{1,0:T(8,128)(2,1)S(1)} %collective-permute-done.10.left, ...), custom_call_target="tpu_custom_call" | custom-call | flops 300000000 | bytes 4000000 | tf_op jit(solution)/shard_map/pallas_call | solution.py:211
  59.4 2.0 %collective-permute-start.15 = (bf16[512,256]{1,0:T(8,128)(2,1)S(1)}, bf16[512,256]{1,0:T(8,128)(2,1)S(1)}, u32[]{:S(2)}, u32[]{:S(2)}) collective-permute-start(bf16[512,256]{1,0:T(8,128)(2,1)S(1)} %shard_map.69), channel_id=1, source_target_pairs={{0,2},{1,3},{2,0},{3,1},{4,6},{5,7},{6,4},{7,5},{8,10},{9,11},{10,... | collective-permute-start | bytes 786440 | tf_op jit(solution)/shard_map/ppermute | solution.py:68
  61.4 1.1 %shard_map.67 = bf16[512,256]{1,0:T(8,128)(2,1)S(1)} custom-call(f32[128,512]{1,0:T(8,128)S(1)} %masks.1, bf16[528,256]{1,0:T(8,128)(2,1)S(1)} %collective-permute-done.12.piece, f32[512,128]{1,0:T(8,128)S(1)} %get-tuple-element.25.spot, f32[512,256]{1,0:T(8,128)S(1)} %get-tuple-element.26.acc, bf16[1040,256]{1,0:T(8,128)(2,1)S(1)} %collective-permute-done.10.left, ...), custom_call_target="tpu_custom_call" | custom-call | flops 300000000 | bytes 4000000 | tf_op jit(solution)/shard_map/pallas_call | solution.py:211
  62.5 2.0 %collective-permute-start.13 = (bf16[512,256]{1,0:T(8,128)(2,1)S(1)}, bf16[512,256]{1,0:T(8,128)(2,1)S(1)}, u32[]{:S(2)}, u32[]{:S(2)}) collective-permute-start(bf16[512,256]{1,0:T(8,128)(2,1)S(1)} %shard_map.67), channel_id=1, source_target_pairs={{0,1},{1,0},{2,3},{3,2},{4,5},{5,4},{6,7},{7,6},{8,9},{9,8},{10,11... | collective-permute-start | bytes 786440 | tf_op jit(solution)/shard_map/ppermute | solution.py:68
  64.5 2.1 %shard_map.64 = (f32[512,128]{1,0:T(8,128)S(1)}, f32[512,256]{1,0:T(8,128)S(1)}) custom-call(f32[128,512]{1,0:T(8,128)S(1)} %masks.1, bf16[528,256]{1,0:T(8,128)(2,1)S(1)} %pack.3.piece, bf16[2,528,256]{2,1,0:T(8,128)(2,1)S(1)} %collective-permute-done.5.oo, bf16[2,512,256]{2,1,0:T(8,128)(2,1)S(1)} %bitcast.9, ...), custom_call_target="tpu_custom_call" | custom-call | flops 1000000000 | bytes 4000000 | tf_op jit(solution)/shard_map/pallas_call | solution.py:185
  66.6 1.1 %shard_map.65.own = f32[512,256]{1,0:T(8,128)S(1)} custom-call(f32[128,512]{1,0:T(8,128)S(1)} %masks.1, bf16[528,256]{1,0:T(8,128)(2,1)S(1)} %pack.3.piece, f32[512,128]{1,0:T(8,128)S(1)} %get-tuple-element.23.spot, f32[512,256]{1,0:T(8,128)S(1)} %get-tuple-element.24.acc, bf16[1040,256]{1,0:T(8,128)(2,1)S(1)} %collective-permute-done.10.left, ...), custom_call_target="tpu_custom_call" | custom-call | flops 300000000 | bytes 4000000 | tf_op jit(solution)/shard_map/pallas_call | solution.py:211
  67.7 4.1 %collective-permute-done.17.x3 = bf16[512,256]{1,0:T(8,128)(2,1)S(1)} collective-permute-done((bf16[512,256]{1,0:T(8,128)(2,1)S(1)}, bf16[512,256]{1,0:T(8,128)(2,1)S(1)}, u32[]{:S(2)}, u32[]{:S(2)}) %collective-permute-start.17) | collective-permute-done | bytes 262176 | tf_op jit(solution)/shard_map/ppermute | solution.py:68
  71.7 1.8 %collective-permute-done.13.x1 = bf16[512,256]{1,0:T(8,128)(2,1)S(1)} collective-permute-done((bf16[512,256]{1,0:T(8,128)(2,1)S(1)}, bf16[512,256]{1,0:T(8,128)(2,1)S(1)}, u32[]{:S(2)}, u32[]{:S(2)}) %collective-permute-start.13) | collective-permute-done | bytes 262176 | tf_op jit(solution)/shard_map/ppermute | solution.py:68
  73.5 0.1 shard_map.72
  73.6 0.4 collective-permute-start.18
  74.0 4.7 %collective-permute-done.18.got = bf16[256,256]{1,0:T(8,128)(2,1)S(1)} collective-permute-done((bf16[256,256]{1,0:T(8,128)(2,1)S(1)}, bf16[256,256]{1,0:T(8,128)(2,1)S(1)}, u32[]{:S(2)}, u32[]{:S(2)}) %collective-permute-start.18) | collective-permute-done | bytes 131104 | tf_op jit(solution)/shard_map/ppermute | solution.py:53
  78.7 6.4 %collective-permute-start.19 = (bf16[64,256]{1,0:T(8,128)(2,1)S(1)}, bf16[64,256]{1,0:T(8,128)(2,1)S(1)}, u32[]{:S(2)}, u32[]{:S(2)}) collective-permute-start(bf16[64,256]{1,0:T(8,128)(2,1)S(1)} %get-tuple-element.34), channel_id=1, source_target_pairs={{0,16},{1,17},{2,18},{3,19},{4,20},{5,21},{6,22},{7,23},{8,24},{9,... | collective-permute-start | bytes 98312 | tf_op jit(solution)/shard_map/ppermute | solution.py:53
  85.1 0.7 collective-permute-start.20
  85.9 1.3 %collective-permute-done.19.z4 = bf16[64,256]{1,0:T(8,128)(2,1)S(1)} collective-permute-done((bf16[64,256]{1,0:T(8,128)(2,1)S(1)}, bf16[64,256]{1,0:T(8,128)(2,1)S(1)}, u32[]{:S(2)}, u32[]{:S(2)}) %collective-permute-start.19) | collective-permute-done | bytes 32800 | tf_op jit(solution)/shard_map/ppermute | solution.py:53
  87.1 3.2 %collective-permute-done.20.z2 = bf16[64,256]{1,0:T(8,128)(2,1)S(1)} collective-permute-done((bf16[64,256]{1,0:T(8,128)(2,1)S(1)}, bf16[64,256]{1,0:T(8,128)(2,1)S(1)}, u32[]{:S(2)}, u32[]{:S(2)}) %collective-permute-start.20) | collective-permute-done | bytes 32800 | tf_op jit(solution)/shard_map/ppermute | solution.py:53
  90.3 1.6 %collective-permute-done.21.z6 = bf16[64,256]{1,0:T(8,128)(2,1)S(1)} collective-permute-done((bf16[64,256]{1,0:T(8,128)(2,1)S(1)}, bf16[64,256]{1,0:T(8,128)(2,1)S(1)}, u32[]{:S(2)}, u32[]{:S(2)}) %collective-permute-start.21) | collective-permute-done | bytes 32800 | tf_op jit(solution)/shard_map/ppermute | solution.py:53
  91.9 0.6 shard_map.74
  (17 shorter events, 0.2 us)
Async XLA Ops:
  0.0 6.6 %copy-start = (bf16[2,1,512,256]{3,2,1,0:T(8,128)(2,1)S(1)}, bf16[2,1,512,256]{3,2,1,0:T(8,128)(2,1)}, u32[]{:S(2)}) copy-start(bf16[2,1,512,256]{3,2,1,0:T(8,128)(2,1)} %param.10) | copy-start | bytes 1572868
  0.0 30.6 %collective-permute-start.7 = (bf16[2,512,256]{2,1,0:T(8,128)(2,1)}, bf16[2,512,256]{2,1,0:T(8,128)(2,1)S(1)}, u32[]{:S(2)}, u32[]{:S(2)}) collective-permute-start(bf16[2,512,256]{2,1,0:T(8,128)(2,1)} %bitcast.4), channel_id=1, source_target_pairs={{0,64},{64,128},{128,192},{192,0},{1,65},{65,129},{129,193},{193,1... | collective-permute-start | bytes 1572872 | tf_op jit(solution)/shard_map/ppermute | solution.py:39
  2.7 3.9 %collective-permute-start = (bf16[80,256]{1,0:T(8,128)(2,1)S(1)}, bf16[80,256]{1,0:T(8,128)(2,1)S(1)}, u32[]{:S(2)}, u32[]{:S(2)}) collective-permute-start(bf16[80,256]{1,0:T(8,128)(2,1)S(1)} %get-tuple-element.21), channel_id=1, source_target_pairs={{0,32},{32,0},{1,33},{33,1},{2,34},{34,2},{3,35},{35,3},{4,36},{36... | collective-permute-start | bytes 122888 | tf_op jit(solution)/shard_map/ppermute | solution.py:35
  2.8 5.4 %collective-permute-start.1 = (bf16[80,256]{1,0:T(8,128)(2,1)S(1)}, bf16[80,256]{1,0:T(8,128)(2,1)S(1)}, u32[]{:S(2)}, u32[]{:S(2)}) collective-permute-start(bf16[80,256]{1,0:T(8,128)(2,1)S(1)} %get-tuple-element.21), channel_id=1, source_target_pairs={{0,36},{1,37},{2,38},{3,39},{4,32},{5,33},{6,34},{7,35},{8,44},{9,... | collective-permute-start | bytes 122888 | tf_op jit(solution)/shard_map/ppermute | solution.py:63
  4.8 26.4 %collective-permute-start.6 = (bf16[2,528,256]{2,1,0:T(8,128)(2,1)S(1)}, bf16[2,528,256]{2,1,0:T(8,128)(2,1)S(1)}, u32[]{:S(2)}, u32[]{:S(2)}) collective-permute-start(bf16[2,528,256]{2,1,0:T(8,128)(2,1)S(1)} %get-tuple-element.22), channel_id=1, source_target_pairs={{0,96},{32,64},{64,160},{96,128},{128,224},{160,192},{192,32},{224... | collective-permute-start | bytes 1622024 | tf_op jit(solution)/shard_map/ppermute | solution.py:48
  5.8 26.9 %collective-permute-start.8 = (bf16[2,528,256]{2,1,0:T(8,128)(2,1)S(1)}, bf16[2,528,256]{2,1,0:T(8,128)(2,1)S(1)}, u32[]{:S(2)}, u32[]{:S(2)}) collective-permute-start(bf16[2,528,256]{2,1,0:T(8,128)(2,1)S(1)} %get-tuple-element.22), channel_id=1, source_target_pairs={{0,224},{32,192},{64,32},{96,0},{128,96},{160,64},{192,160},{224,1... | collective-permute-start | bytes 1622024 | tf_op jit(solution)/shard_map/ppermute | solution.py:48
  6.6 26.1 %collective-permute-start.9 = (bf16[2,512,256]{2,1,0:T(8,128)(2,1)S(1)}, bf16[2,512,256]{2,1,0:T(8,128)(2,1)S(1)}, u32[]{:S(2)}, u32[]{:S(2)}) collective-permute-start(bf16[2,512,256]{2,1,0:T(8,128)(2,1)S(1)} %bitcast.5), channel_id=1, source_target_pairs={{0,192},{64,0},{128,64},{192,128},{1,193},{65,1},{129,65},{193,129... | collective-permute-start | bytes 1572872 | tf_op jit(solution)/shard_map/ppermute | solution.py:39
  8.3 9.8 %collective-permute-start.2 = (bf16[144,256]{1,0:T(8,128)(2,1)S(1)}, bf16[144,256]{1,0:T(8,128)(2,1)S(1)}, u32[]{:S(2)}, u32[]{:S(2)}) collective-permute-start(bf16[144,256]{1,0:T(8,128)(2,1)S(1)} %pack.2.refs_0_), channel_id=1, source_target_pairs={{0,16},{1,17},{2,18},{3,19},{4,20},{5,21},{6,22},{7,23},{8,24},{9,... | collective-permute-start | bytes 221192 | tf_op jit(solution)/shard_map/ppermute | solution.py:53
  18.0 6.0 %collective-permute-start.3 = (bf16[144,256]{1,0:T(8,128)(2,1)S(1)}, bf16[144,256]{1,0:T(8,128)(2,1)S(1)}, u32[]{:S(2)}, u32[]{:S(2)}) collective-permute-start(bf16[144,256]{1,0:T(8,128)(2,1)S(1)} %pack.2.refs_0_), channel_id=1, source_target_pairs={{0,8},{1,9},{2,10},{3,11},{4,12},{5,13},{6,14},{7,15},{8,0},{9,1},... | collective-permute-start | bytes 221192 | tf_op jit(solution)/shard_map/ppermute | solution.py:53
  24.1 6.5 %collective-permute-start.4 = (bf16[144,256]{1,0:T(8,128)(2,1)S(1)}, bf16[144,256]{1,0:T(8,128)(2,1)S(1)}, u32[]{:S(2)}, u32[]{:S(2)}) collective-permute-start(bf16[144,256]{1,0:T(8,128)(2,1)S(1)} %pack.2.refs_0_), channel_id=1, source_target_pairs={{0,24},{1,25},{2,26},{3,27},{4,28},{5,29},{6,30},{7,31},{8,16},{9,... | collective-permute-start | bytes 221192 | tf_op jit(solution)/shard_map/ppermute | solution.py:53
  30.6 16.4 %collective-permute-start.5 = (bf16[2,528,256]{2,1,0:T(8,128)(2,1)S(1)}, bf16[2,528,256]{2,1,0:T(8,128)(2,1)S(1)}, u32[]{:S(2)}, u32[]{:S(2)}) collective-permute-start(bf16[2,528,256]{2,1,0:T(8,128)(2,1)S(1)} %get-tuple-element.22), channel_id=1, source_target_pairs={{0,32},{32,0},{1,33},{33,1},{2,34},{34,2},{3,35},{35,3},{4,36},{36... | collective-permute-start | bytes 1622024 | tf_op jit(solution)/shard_map/ppermute | solution.py:35
  30.7 16.0 %collective-permute-start.16 = (bf16[528,256]{1,0:T(8,128)(2,1)S(1)}, bf16[528,256]{1,0:T(8,128)(2,1)S(1)}, u32[]{:S(2)}, u32[]{:S(2)}) collective-permute-start(bf16[528,256]{1,0:T(8,128)(2,1)S(1)} %pack.3.piece), channel_id=1, source_target_pairs={{0,3},{1,2},{2,1},{3,0},{4,7},{5,6},{6,5},{7,4},{8,11},{9,10},{10,... | collective-permute-start | bytes 811016 | tf_op jit(solution)/shard_map/ppermute | solution.py:68
  31.3 15.4 %copy-start.1 = (s32[2,512,16]{1,2,0:T(8,128)S(1)}, s32[2,512,16]{1,2,0:T(8,128)}, u32[]{:S(2)}) copy-start(s32[2,512,16]{1,2,0:T(8,128)} %param.11) | copy-start | bytes 196612
  31.3 25.5 %collective-permute-start.10 = (bf16[1040,256]{1,0:T(8,128)(2,1)S(1)}, bf16[1040,256]{1,0:T(8,128)(2,1)S(1)}, u32[]{:S(2)}, u32[]{:S(2)}) collective-permute-start(bf16[1040,256]{1,0:T(8,128)(2,1)S(1)} %relay.2), channel_id=1, source_target_pairs={{0,64},{64,128},{128,192},{192,0},{1,65},{65,129},{129,193},{193,1... | collective-permute-start | bytes 1597448 | tf_op jit(solution)/shard_map/ppermute | solution.py:39
  32.7 24.0 %collective-permute-start.11 = (bf16[1040,256]{1,0:T(8,128)(2,1)S(1)}, bf16[1040,256]{1,0:T(8,128)(2,1)S(1)}, u32[]{:S(2)}, u32[]{:S(2)}) collective-permute-start(bf16[1040,256]{1,0:T(8,128)(2,1)S(1)} %relay.3), channel_id=1, source_target_pairs={{0,192},{64,0},{128,64},{192,128},{1,193},{65,1},{129,65},{193,129... | collective-permute-start | bytes 1597448 | tf_op jit(solution)/shard_map/ppermute | solution.py:39
  33.5 15.5 %collective-permute-start.14 = (bf16[528,256]{1,0:T(8,128)(2,1)S(1)}, bf16[528,256]{1,0:T(8,128)(2,1)S(1)}, u32[]{:S(2)}, u32[]{:S(2)}) collective-permute-start(bf16[528,256]{1,0:T(8,128)(2,1)S(1)} %pack.3.piece), channel_id=1, source_target_pairs={{0,2},{1,3},{2,0},{3,1},{4,6},{5,7},{6,4},{7,5},{8,10},{9,11},{10,... | collective-permute-start | bytes 811016 | tf_op jit(solution)/shard_map/ppermute | solution.py:68
  46.6 8.0 %collective-permute-start.12 = (bf16[528,256]{1,0:T(8,128)(2,1)S(1)}, bf16[528,256]{1,0:T(8,128)(2,1)S(1)}, u32[]{:S(2)}, u32[]{:S(2)}) collective-permute-start(bf16[528,256]{1,0:T(8,128)(2,1)S(1)} %pack.3.piece), channel_id=1, source_target_pairs={{0,1},{1,0},{2,3},{3,2},{4,5},{5,4},{6,7},{7,6},{8,9},{9,8},{10,11... | collective-permute-start | bytes 811016 | tf_op jit(solution)/shard_map/ppermute | solution.py:68
  57.8 13.9 %collective-permute-start.17 = (bf16[512,256]{1,0:T(8,128)(2,1)S(1)}, bf16[512,256]{1,0:T(8,128)(2,1)S(1)}, u32[]{:S(2)}, u32[]{:S(2)}) collective-permute-start(bf16[512,256]{1,0:T(8,128)(2,1)S(1)} %shard_map.71), channel_id=1, source_target_pairs={{0,3},{1,2},{2,1},{3,0},{4,7},{5,6},{6,5},{7,4},{8,11},{9,10},{10,... | collective-permute-start | bytes 786440 | tf_op jit(solution)/shard_map/ppermute | solution.py:68
  59.4 12.3 %collective-permute-start.15 = (bf16[512,256]{1,0:T(8,128)(2,1)S(1)}, bf16[512,256]{1,0:T(8,128)(2,1)S(1)}, u32[]{:S(2)}, u32[]{:S(2)}) collective-permute-start(bf16[512,256]{1,0:T(8,128)(2,1)S(1)} %shard_map.69), channel_id=1, source_target_pairs={{0,2},{1,3},{2,0},{3,1},{4,6},{5,7},{6,4},{7,5},{8,10},{9,11},{10,... | collective-permute-start | bytes 786440 | tf_op jit(solution)/shard_map/ppermute | solution.py:68
  62.5 11.0 %collective-permute-start.13 = (bf16[512,256]{1,0:T(8,128)(2,1)S(1)}, bf16[512,256]{1,0:T(8,128)(2,1)S(1)}, u32[]{:S(2)}, u32[]{:S(2)}) collective-permute-start(bf16[512,256]{1,0:T(8,128)(2,1)S(1)} %shard_map.67), channel_id=1, source_target_pairs={{0,1},{1,0},{2,3},{3,2},{4,5},{5,4},{6,7},{7,6},{8,9},{9,8},{10,11... | collective-permute-start | bytes 786440 | tf_op jit(solution)/shard_map/ppermute | solution.py:68
  73.6 5.1 %collective-permute-start.18 = (bf16[256,256]{1,0:T(8,128)(2,1)S(1)}, bf16[256,256]{1,0:T(8,128)(2,1)S(1)}, u32[]{:S(2)}, u32[]{:S(2)}) collective-permute-start(bf16[256,256]{1,0:T(8,128)(2,1)S(1)} %get-tuple-element.32), channel_id=1, source_target_pairs={{0,4},{1,5},{2,6},{3,7},{4,0},{5,1},{6,2},{7,3},{8,12},{9,13},{10,... | collective-permute-start | bytes 393224 | tf_op jit(solution)/shard_map/ppermute | solution.py:53
  78.7 8.4 %collective-permute-start.19 = (bf16[64,256]{1,0:T(8,128)(2,1)S(1)}, bf16[64,256]{1,0:T(8,128)(2,1)S(1)}, u32[]{:S(2)}, u32[]{:S(2)}) collective-permute-start(bf16[64,256]{1,0:T(8,128)(2,1)S(1)} %get-tuple-element.34), channel_id=1, source_target_pairs={{0,16},{1,17},{2,18},{3,19},{4,20},{5,21},{6,22},{7,23},{8,24},{9,... | collective-permute-start | bytes 98312 | tf_op jit(solution)/shard_map/ppermute | solution.py:53
  85.1 5.2 %collective-permute-start.20 = (bf16[64,256]{1,0:T(8,128)(2,1)S(1)}, bf16[64,256]{1,0:T(8,128)(2,1)S(1)}, u32[]{:S(2)}, u32[]{:S(2)}) collective-permute-start(bf16[64,256]{1,0:T(8,128)(2,1)S(1)} %get-tuple-element.35), channel_id=1, source_target_pairs={{0,8},{1,9},{2,10},{3,11},{4,12},{5,13},{6,14},{7,15},{8,0},{9,1},... | collective-permute-start | bytes 98312 | tf_op jit(solution)/shard_map/ppermute | solution.py:53
  85.9 6.0 %collective-permute-start.21 = (bf16[64,256]{1,0:T(8,128)(2,1)S(1)}, bf16[64,256]{1,0:T(8,128)(2,1)S(1)}, u32[]{:S(2)}, u32[]{:S(2)}) collective-permute-start(bf16[64,256]{1,0:T(8,128)(2,1)S(1)} %get-tuple-element.36), channel_id=1, source_target_pairs={{0,24},{1,25},{2,26},{3,27},{4,28},{5,29},{6,30},{7,31},{8,16},{9,... | collective-permute-start | bytes 98312 | tf_op jit(solution)/shard_map/ppermute | solution.py:53
